TPU v7x, 32 devices: a whole 2x2x4 slice. The times are simulated.
32 devices in a mesh: rep: 2 (over y), shard: 16 (over z, x, core).
Axes of the slice: x: 2, y: 2, z: 4, core: 2. Of those that a mesh axis runs over, the one named last changes fastest.
Arguments:
- block_input: bfloat16 [32768, 768], P(('rep', 'shard')), may hold values from -6 to 6
- history: bfloat16 [4, 32768, 768], P(None, ('rep', 'shard')), may hold values from -6 to 6
- cotangent: bfloat16 [32768, 768], P(('rep', 'shard')), may hold values from -6 to 6
- span_start: int32 [32], P(('rep', 'shard')), may hold values from 0 to 768, as said below
- w_qkv: bfloat16 [768, 2304], P('shard'), may hold values from -0.21875 to 0.21875
- w_out: bfloat16 [768, 768], P('shard'), may hold values from -4 to 4
- w_up: bfloat16 [768, 3072], P('shard'), may hold values from -0.21875 to 0.21875
- w_down: bfloat16 [3072, 768], P('shard'), may hold values from -0.109375 to 0.109375
- ln_gains: bfloat16 [2, 768], P(None, 'shard'), may hold values from 0.5 to 1.5
- ln_biases: bfloat16 [2, 768], P(None, 'shard'), may hold values from -3 to 3
- mix_weights: float32 [5], replicated, may hold values from 0.3 to 1
Outputs:
- next_input: bfloat16 [32768, 768], P(('rep', 'shard'))
- grad_input: float32 [32768, 768], P(('rep', 'shard'))
- grad_history: float32 [4, 32768, 768], P(None, ('rep', 'shard'))
- grad_mix: float32 [5], replicated
- grad_w_qkv: float32 [768, 2304], P('shard')
- grad_w_out: float32 [768, 768], P('shard')
- grad_w_up: float32 [768, 3072], P('shard')
- grad_w_down: float32 [3072, 768], P('shard')
- grad_gains: float32 [2, 768], P(None, 'shard')
- grad_bias_first: float32 [768], P('shard')
- grad_bias_second: float32 [768], P('shard')
Inputs may be any that keep to these rules, and one draw needn't show every extreme that they name: Sequence n's picture span covers positions span_start[n] to span_start[n] + 255 of that sequence.
All inputs are finite; a program needn't handle non-finite values.
Results may differ from a plain program's by a relative error of at most 0.017.
Values may be sent and summed in bfloat16 or wider, within the bound.
A program may use at most 256 MiB of HBM per device.

v0:
```python
import jax
import jax.numpy as jnp
from jax import lax
from jax.sharding import PartitionSpec as P

HEADS = 12
SPAN = 256
eps = 1e-05


def layer_norm(values, gain_row, bias_row):
    average = jnp.mean(values, axis=-1, keepdims=True)
    centered = values - average
    inverse_std = lax.rsqrt(jnp.mean(centered * centered, axis=-1, keepdims=True) + eps)
    normed = centered * inverse_std
    return (normed * gain_row + bias_row, normed, inverse_std)


def layer_norm_back(incoming, normed, inverse_std, gain_row):
    scaled = incoming * gain_row
    inner = (
        scaled
        - jnp.mean(scaled, axis=-1, keepdims=True)
        - normed * jnp.mean(scaled * normed, axis=-1, keepdims=True)
    )
    return (inverse_std * inner, jnp.sum(incoming * normed, axis=0), jnp.sum(incoming, axis=0))


def rotary_tables(length, head_width):
    half_width = head_width // 2
    frequency = jnp.exp(
        -jnp.log(10000.0) * jnp.arange(half_width, dtype=jnp.float32) * (2.0 / head_width)
    )
    angles = jnp.arange(length, dtype=jnp.float32)[:, None] * frequency[None, :]
    angles = jnp.concatenate([angles, angles], axis=-1)[:, None, :]
    return (jnp.cos(angles), jnp.sin(angles))


def rotate(values, cosine, sine):
    half_width = values.shape[-1] // 2
    turned = jnp.concatenate([-values[..., half_width:], values[..., :half_width]], axis=-1)
    return values * cosine + turned * sine


def rotate_back(incoming, cosine, sine):
    half_width = incoming.shape[-1] // 2
    weighted = incoming * sine
    turned = jnp.concatenate([weighted[..., half_width:], -weighted[..., :half_width]], axis=-1)
    return incoming * cosine + turned


def gelu_parts(upper):
    normal_cdf = 0.5 * (1.0 + lax.erf(upper * 0.7071067811865476))
    density = jnp.exp(-0.5 * upper * upper) * 0.3989422804014327
    return (upper * normal_cdf, normal_cdf + upper * density)


def visible(row_pos, col_pos, span_begin):
    row_in = (row_pos >= span_begin) & (row_pos < span_begin + SPAN)
    col_in = (col_pos >= span_begin) & (col_pos < span_begin + SPAN)
    return (col_pos[None, :] <= row_pos[:, None]) | row_in[:, None] & col_in[None, :]


def block_scores(query_block, key_rows, row_pos, col_pos, span_begin):
    factor = query_block.shape[2] ** (-0.5)
    scores = (
        jnp.einsum("qhd,khd->hqk", query_block, key_rows, preferred_element_type=jnp.float32)
        * factor
    )
    return jnp.where(visible(row_pos, col_pos, span_begin)[None], scores, -1e30)


def attend_forward(query_rows, key_rows, value_rows, span_begin):
    length = query_rows.shape[0]
    block_rows = min(512, length)
    block_count = length // block_rows
    col_pos = jnp.arange(length, dtype=jnp.int32)

    def one_block(block_index):
        first_row = block_index * block_rows
        row_pos = first_row + jnp.arange(block_rows, dtype=jnp.int32)
        query_block = lax.dynamic_slice_in_dim(query_rows, first_row, block_rows, 0)
        scores = block_scores(query_block, key_rows, row_pos, col_pos, span_begin)
        row_max = jnp.max(scores, axis=-1, keepdims=True)
        log_sums = row_max + jnp.log(jnp.sum(jnp.exp(scores - row_max), axis=-1, keepdims=True))
        attn_probs = jnp.exp(scores - log_sums).astype(jnp.bfloat16)
        block_out = jnp.einsum(
            "hqk,khd->qhd", attn_probs, value_rows, preferred_element_type=jnp.float32
        )
        return (block_out.astype(jnp.bfloat16), log_sums[..., 0])

    outputs, log_sums = lax.map(one_block, jnp.arange(block_count, dtype=jnp.int32))
    return (outputs.reshape(query_rows.shape), log_sums)


def attend_backward(query_rows, key_rows, value_rows, grad_rows, log_sums, span_begin):
    length = query_rows.shape[0]
    block_rows = min(512, length)
    block_count = length // block_rows
    col_pos = jnp.arange(length, dtype=jnp.int32)
    factor = query_rows.shape[2] ** (-0.5)

    def one_block(running, block_index):
        grad_keys, grad_values = running
        first_row = block_index * block_rows
        row_pos = first_row + jnp.arange(block_rows, dtype=jnp.int32)
        query_block = lax.dynamic_slice_in_dim(query_rows, first_row, block_rows, 0)
        grad_block = lax.dynamic_slice_in_dim(grad_rows, first_row, block_rows, 0)
        scores = block_scores(query_block, key_rows, row_pos, col_pos, span_begin)
        attn_probs = jnp.exp(scores - log_sums[block_index][..., None])
        grad_probs = jnp.einsum(
            "qhd,khd->hqk", grad_block, value_rows, preferred_element_type=jnp.float32
        )
        delta_sum = jnp.sum(attn_probs * grad_probs, axis=-1, keepdims=True)
        grad_scores = (attn_probs * (grad_probs - delta_sum)).astype(jnp.bfloat16)
        grad_query = (
            jnp.einsum("hqk,khd->qhd", grad_scores, key_rows, preferred_element_type=jnp.float32)
            * factor
        )
        grad_keys = (
            grad_keys
            + jnp.einsum(
                "hqk,qhd->khd", grad_scores, query_block, preferred_element_type=jnp.float32
            )
            * factor
        )
        grad_values = grad_values + jnp.einsum(
            "hqk,qhd->khd",
            attn_probs.astype(jnp.bfloat16),
            grad_block,
            preferred_element_type=jnp.float32,
        )
        return ((grad_keys, grad_values), grad_query)

    zero_rows = jnp.zeros(key_rows.shape, jnp.float32)
    (grad_keys, grad_values), grad_queries = lax.scan(
        one_block, (zero_rows, zero_rows), jnp.arange(block_count, dtype=jnp.int32)
    )
    return (grad_queries.reshape(query_rows.shape), grad_keys, grad_values)


def local(
    block_input,
    history,
    cotangent,
    span_start,
    w_qkv,
    w_out,
    w_up,
    w_down,
    ln_gains,
    ln_biases,
    mix_weights,
):
    tokens, model_width = block_input.shape
    seq_count = span_start.shape[0]
    length = tokens // seq_count
    head_count = HEADS
    head_width = model_width // head_count
    past_count = history.shape[0]
    full_qkv, full_out, full_up, full_down, gains_low, biases_low = (
        lax.all_gather(w_qkv, "shard", axis=0, tiled=True),
        lax.all_gather(w_out, "shard", axis=0, tiled=True),
        lax.all_gather(w_up, "shard", axis=0, tiled=True),
        lax.all_gather(w_down, "shard", axis=0, tiled=True),
        lax.all_gather(ln_gains, "shard", axis=1, tiled=True),
        lax.all_gather(ln_biases, "shard", axis=1, tiled=True),
    )
    gains = gains_low.astype(jnp.float32)
    biases = biases_low.astype(jnp.float32)
    inputs_f = block_input.astype(jnp.float32)
    normed1_out, normed1, inverse1 = layer_norm(inputs_f, gains[0], biases[0])
    act1 = normed1_out.astype(jnp.bfloat16)
    projected = jnp.dot(act1, full_qkv, preferred_element_type=jnp.float32)
    cosine, sine = rotary_tables(length, head_width)
    split_shape = (seq_count, length, head_count, head_width)
    q_rot = rotate(projected[:, :model_width].reshape(split_shape), cosine, sine).astype(
        jnp.bfloat16
    )
    k_rot = rotate(
        projected[:, model_width : 2 * model_width].reshape(split_shape), cosine, sine
    ).astype(jnp.bfloat16)
    v_low = projected[:, 2 * model_width :].reshape(split_shape).astype(jnp.bfloat16)

    def forward_sequence(inputs_now):
        query_rows, key_rows, value_rows, span_begin = inputs_now
        return attend_forward(query_rows, key_rows, value_rows, span_begin)

    mixed, log_sums = lax.map(forward_sequence, (q_rot, k_rot, v_low, span_start))
    mixed = mixed.reshape(tokens, model_width)
    middle = inputs_f + jnp.dot(mixed, full_out, preferred_element_type=jnp.float32)
    normed2_out, normed2, inverse2 = layer_norm(middle, gains[1], biases[1])
    act2 = normed2_out.astype(jnp.bfloat16)
    upper = jnp.dot(act2, full_up, preferred_element_type=jnp.float32)
    activated, slope = gelu_parts(upper)
    hidden = activated.astype(jnp.bfloat16)
    output = middle + jnp.dot(hidden, full_down, preferred_element_type=jnp.float32)
    earlier = jnp.einsum("k,ktd->td", mix_weights[:past_count], history.astype(jnp.float32))
    next_input = (earlier + mix_weights[past_count] * output).astype(jnp.bfloat16)
    grad_f = cotangent.astype(jnp.float32)
    grad_history = mix_weights[:past_count][:, None, None] * grad_f[None]
    history_terms = jnp.einsum("ktd,td->k", history, cotangent, preferred_element_type=jnp.float32)
    partial_mix = jnp.concatenate([history_terms, jnp.sum(grad_f * output)[None]])
    grad_mix = lax.psum(partial_mix, ("rep", "shard"))
    full_qkv, full_out, full_up, full_down = (
        lax.all_gather(w_qkv, "shard", axis=0, tiled=True),
        lax.all_gather(w_out, "shard", axis=0, tiled=True),
        lax.all_gather(w_up, "shard", axis=0, tiled=True),
        lax.all_gather(w_down, "shard", axis=0, tiled=True),
    )
    grad_output = mix_weights[past_count] * grad_f
    grad_branch = grad_output.astype(jnp.bfloat16)
    grad_w_down = jnp.einsum("tf,td->fd", hidden, grad_branch, preferred_element_type=jnp.float32)
    grad_hidden = jnp.einsum(
        "td,fd->tf", grad_branch, full_down, preferred_element_type=jnp.float32
    )
    grad_upper = (grad_hidden * slope).astype(jnp.bfloat16)
    grad_w_up = jnp.einsum("td,tf->df", act2, grad_upper, preferred_element_type=jnp.float32)
    grad_act2 = jnp.einsum("tf,df->td", grad_upper, full_up, preferred_element_type=jnp.float32)
    grad_norm2, grad_gain2, grad_bias2 = layer_norm_back(grad_act2, normed2, inverse2, gains[1])
    grad_middle = grad_output + grad_norm2
    grad_attended = grad_middle.astype(jnp.bfloat16)
    grad_w_out = jnp.einsum("ti,tj->ij", mixed, grad_attended, preferred_element_type=jnp.float32)
    grad_mixed = jnp.einsum(
        "tj,ij->ti", grad_attended, full_out, preferred_element_type=jnp.float32
    ).astype(jnp.bfloat16)

    def backward_sequence(inputs_now):
        query_rows, key_rows, value_rows, grad_rows, sums_now, span_begin = inputs_now
        return attend_backward(query_rows, key_rows, value_rows, grad_rows, sums_now, span_begin)

    grad_q, grad_k, grad_v = lax.map(
        backward_sequence,
        (q_rot, k_rot, v_low, grad_mixed.reshape(split_shape), log_sums, span_start),
    )
    grad_q = rotate_back(grad_q, cosine, sine).reshape(tokens, model_width)
    grad_k = rotate_back(grad_k, cosine, sine).reshape(tokens, model_width)
    grad_projected = jnp.concatenate(
        [grad_q, grad_k, grad_v.reshape(tokens, model_width)], axis=1
    ).astype(jnp.bfloat16)
    grad_w_qkv = jnp.einsum("ti,tj->ij", act1, grad_projected, preferred_element_type=jnp.float32)
    grad_act1 = jnp.einsum(
        "tj,ij->ti", grad_projected, full_qkv, preferred_element_type=jnp.float32
    )
    grad_norm1, grad_gain1, grad_bias1 = layer_norm_back(grad_act1, normed1, inverse1, gains[0])
    grad_input = grad_middle + grad_norm1
    grad_gains = jnp.stack([grad_gain1, grad_gain2])
    grad_biases = jnp.stack([grad_bias1, grad_bias2])
    local_grads = (grad_w_qkv, grad_w_out, grad_w_up, grad_w_down, grad_gains, grad_biases)
    owned = (
        lax.psum_scatter(
            local_grads[0].astype(jnp.bfloat16), "shard", scatter_dimension=0, tiled=True
        ).astype(jnp.float32),
        lax.psum_scatter(
            local_grads[1].astype(jnp.bfloat16), "shard", scatter_dimension=0, tiled=True
        ).astype(jnp.float32),
        lax.psum_scatter(
            local_grads[2].astype(jnp.bfloat16), "shard", scatter_dimension=0, tiled=True
        ).astype(jnp.float32),
        lax.psum_scatter(
            local_grads[3].astype(jnp.bfloat16), "shard", scatter_dimension=0, tiled=True
        ).astype(jnp.float32),
        lax.psum_scatter(
            local_grads[4].astype(jnp.bfloat16), "shard", scatter_dimension=1, tiled=True
        ).astype(jnp.float32),
        lax.psum_scatter(
            local_grads[5].astype(jnp.bfloat16), "shard", scatter_dimension=1, tiled=True
        ).astype(jnp.float32),
    )
    owned = (
        lax.psum(owned[0].astype(jnp.bfloat16), "rep").astype(jnp.float32),
        lax.psum(owned[1].astype(jnp.bfloat16), "rep").astype(jnp.float32),
        lax.psum(owned[2].astype(jnp.bfloat16), "rep").astype(jnp.float32),
        lax.psum(owned[3].astype(jnp.bfloat16), "rep").astype(jnp.float32),
        lax.psum(owned[4].astype(jnp.bfloat16), "rep").astype(jnp.float32),
        lax.psum(owned[5].astype(jnp.bfloat16), "rep").astype(jnp.float32),
    )
    return (
        next_input,
        grad_input,
        grad_history,
        grad_mix,
        owned[0],
        owned[1],
        owned[2],
        owned[3],
        owned[4],
        owned[5][0],
        owned[5][1],
    )


def solution(mesh):
    placed = (
        P(("rep", "shard"), None),
        P(None, ("rep", "shard"), None),
        P(("rep", "shard"), None),
        P(("rep", "shard")),
        P("shard", None),
        P("shard", None),
        P("shard", None),
        P("shard", None),
        P(None, "shard"),
        P(None, "shard"),
        P(),
    )
    return jax.shard_map(
        local,
        mesh=mesh,
        in_specs=placed,
        out_specs=(
            P(("rep", "shard"), None),
            P(("rep", "shard"), None),
            P(None, ("rep", "shard"), None),
            P(),
            P("shard", None),
            P("shard", None),
            P("shard", None),
            P("shard", None),
            P(None, "shard"),
            P("shard"),
            P("shard"),
        ),
        check_vma=False,
    )
```

profile of v0, /device:TPU:0, one launch (start us, length us, event | category | flops | bytes accessed | tf_op | source)
XLA Modules:
  0.0 911.4 jit_solution(13864573590740779968)
XLA Ops:
  12.0 23.4 %all-gather = bf16[16,48,2]{1,2,0:T(2,128)(2,1)S(1)} all-gather(bf16[1,48,2]{1,2,0:T(2,128)(2,1)} %bitcast.170), channel_id=1, replica_groups=mesh['rep'=2,'shard'=16] {'shard'}, dimensions={0}, use_global_device_ids=true | all-gather | bytes 3264 | tf_op jit(solution)/shard_map/all_gather | solution.py:166
  35.5 17.7 %all-gather.1 = bf16[16,48,2]{1,2,0:T(2,128)(2,1)S(1)} all-gather(bf16[1,48,2]{1,2,0:T(2,128)(2,1)} %bitcast.171), channel_id=1, replica_groups=mesh['rep'=2,'shard'=16] {'shard'}, dimensions={0}, use_global_device_ids=true | all-gather | bytes 3264 | tf_op jit(solution)/shard_map/all_gather | solution.py:167
  106.9 78.3 %while.52 = (s32[]{:T(128)}, bf16[2,512,12,64]{1,3,2,0:T(8,128)(2,1)S(1)}, f32[2,12,512]{2,1,0:T(8,128)S(1)}, s32[2]{0:T(128)S(1)}, s32[]{:T(128)}, /*index=5*/s...) while((s32[]{:T(128)}, ...), condition=%wide.region_5.6_spmd.clone.clone, body=%wide.region_2.5_spmd.clone.clone.sunk | while | flops 1681784320 | bytes 82558176 | solution.py:92
  109.9 12.0 %fusion.130 = (f32[12,512]{1,0:T(8,128)S(1)}, f32[12,512,1024]{2,1,0:T(8,128)}) fusion(pred[512,1024]{1,0:T(8,128)(4,1)S(1)} %fusion.129, bf16[1024,12,64]{0,2,1:T(8,128)(2,1)S(1)} %get-tuple-element.733, bf16[1024,12,64]{0,2,1:T(8,128)(2,1)} %get-tuple-element.732, s32[]{:T(128)S(6)} %select_n.68), kind=kOutput, calls=%fused_computation.5.clone.1 | convolution fusion | flops 824174592 | bytes 28073988 | tf_op jit(solution)/shard_map/while/body/eval_jaxpr/while/body/eval_jaxpr/qhd,khd->hqk/dot_general | solution.py:67
  122.0 12.3 %exponential_reduce_fusion.2 = f32[12,512]{1,0:T(8,128)S(1)} fusion(f32[12,512,1024]{2,1,0:T(8,128)} %get-tuple-element.682, f32[12,512]{1,0:T(8,128)S(1)} %get-tuple-element.683, pred[512,1024]{1,0:T(8,128)(4,1)S(1)} %fusion.129), kind=kLoop, calls=%fused_computation.3.clone.1 | loop fusion | flops 25159680 | bytes 25739264 | tf_op jit(solution)/shard_map/while/body/eval_jaxpr/while/body/eval_jaxpr/reduce_sum | solution.py:85
  149.1 12.0 %fusion.130 = (f32[12,512]{1,0:T(8,128)S(1)}, f32[12,512,1024]{2,1,0:T(8,128)}) fusion(pred[512,1024]{1,0:T(8,128)(4,1)S(1)} %fusion.129, bf16[1024,12,64]{0,2,1:T(8,128)(2,1)S(1)} %get-tuple-element.733, bf16[1024,12,64]{0,2,1:T(8,128)(2,1)} %get-tuple-element.732, s32[]{:T(128)S(6)} %select_n.68), kind=kOutput, calls=%fused_computation.5.clone.1 | convolution fusion | flops 824174592 | bytes 28073988 | tf_op jit(solution)/shard_map/while/body/eval_jaxpr/while/body/eval_jaxpr/qhd,khd->hqk/dot_general | solution.py:67
  196.5 13.6 %multiply_convert_fusion.1 = (bf16[1024,3072]{1,0:T(8,128)(2,1)}, f32[1024,3072]{1,0:T(8,128)}) fusion(bf16[768,3072]{1,0:T(8,128)(2,1)} %all-gather.11.cloned.1.call-done, f32[1024,768]{0,1:T(8,128)} %copy-done.8, f32[768]{0:T(1024)S(1)} %copy-done.45, f32[768]{0:T(1024)S(1)} %copy-done.40, f32[1024]{0:T(1024)S(1)} %add_rsqrt_fusion, ...), kind=kOutput, calls=%fused_computation.62 | convolution fusion | flops 4851499008 | bytes 26753024 | tf_op jit(solution)/shard_map/dot_general | solution.py:194
  210.1 12.8 %fusion.42 = bf16[1024,3072]{1,0:T(8,128)(2,1)S(1)} fusion(f32[1024,3072]{1,0:T(8,128)} %get-tuple-element.553, bf16[3072,768]{1,0:T(8,128)(2,1)} %all-gather.13.cloned.1.call-done, bf16[1024,768]{0,1:T(8,128)(2,1)S(1)} %copy-done.16, f32[]{:T(128)} %bitcast.4), kind=kOutput, calls=%fused_computation.60 | convolution fusion | flops 4865654784 | bytes 25165828 | tf_op jit(solution)/shard_map/td,fd->tf/dot_general | solution.py:214
  238.5 12.5 %multiply_reduce_fusion.3 = (f32[]{:T(128)}, bf16[1024,768]{0,1:T(8,128)(2,1)}, f32[1024,768]{0,1:T(8,128)S(1)}) fusion(bf16[1024,768]{0,1:T(8,128)(2,1)S(1)} %copy-done.16, f32[]{:T(128)} %bitcast.4, f32[1,1024,768]{1,2,0:T(8,128)} %copy.101, f32[1024]{0:T(1024)S(1)} %broadcast_multiply_fusion.4, f32[1024,768]{0,1:T(8,128)S(1)} %copy-done.9, ...), kind=kOutput, calls=%fused_computation.104 | convolution fusion | flops 4844421120 | bytes 26758152 | tf_op jit(solution)/shard_map/dot_general | solution.py:197
  261.1 239.0 %while.53 = (s32[]{:T(128)}, f32[1024,12,64]{0,2,1:T(8,128)}, f32[1024,12,64]{0,2,1:T(8,128)}, f32[2,512,12,64]{1,0,3,2:T(2,128)}, s32[2]{0:T(128)S(1)}, /*index...) while((s32[]{:T(128)}, f32[1024,12,64]{0,2,1:T(8,128)}, ...), condition=%wide.region_12.13_spmd.clone.clone, body=%wide.region_10.12_spmd.clone.clone.sunk | while | flops 4126801408 | bytes 231923056 | solution.py:136
  278.2 13.5 %bitcast_add_fusion.7 = f32[1024,12,64]{0,2,1:T(8,128)} fusion(f32[1024,12,64]{0,2,1:T(8,128)} %get-tuple-element.758, f32[12,512,1024]{2,1,0:T(8,128)} %fusion.141, f32[12,512]{1,0:T(8,128)S(1)} %dynamic-slice_bitcast_fusion.2, pred[512,1024]{1,0:T(8,128)(4,1)S(1)} %fusion.143, pred[]{:T(512)S(6)} %compare.3, ...), kind=kOutput, calls=%fused_computation.31.clone.1 | convolution fusion | flops 832045056 | bytes 32800772 | tf_op jit(solution)/shard_map/while/body/eval_jaxpr/while/body/eval_jaxpr/hqk,qhd->khd/dot_general | solution.py:127
  291.7 18.2 %multiply_reduce_fusion.9 = (f32[12,512]{1,0:T(8,128)S(1)}, f32[12,512,1024]{2,1,0:T(8,128)}) fusion(f32[12,512,1024]{2,1,0:T(8,128)} %fusion.141, f32[12,512]{1,0:T(8,128)S(1)} %dynamic-slice_bitcast_fusion.2, pred[512,1024]{1,0:T(8,128)(4,1)S(1)} %fusion.143, bf16[1024,12,64]{0,2,1:T(8,128)(2,1)} %get-tuple-element.784, ...), kind=kOutput, calls=%fused_computation.26.clone.1 | convolution fusion | flops 836757504 | bytes 53264388 | tf_op jit(solution)/shard_map/while/body/eval_jaxpr/while/body/eval_jaxpr/qhd,khd->hqk/dot_general | solution.py:111
  309.9 21.3 %multiply_convert_fusion.6 = bf16[12,512,1024]{2,1,0:T(8,128)(2,1)} fusion(f32[12,512,1024]{2,1,0:T(8,128)} %get-tuple-element.698, f32[12,512,1024]{2,1,0:T(8,128)} %fusion.141, f32[12,512]{1,0:T(8,128)S(1)} %get-tuple-element.699, f32[12,512]{1,0:T(8,128)S(1)} %dynamic-slice_bitcast_fusion.2, pred[512,1024]{1,0:T(8,128)(4,1)S(1)} %fusion.143), kind=kLoop, calls=%fused_computation.25.clone.1 | loop fusion | flops 37748736 | bytes 63488000 | tf_op jit(solution)/shard_map/while/body/eval_jaxpr/while/body/eval_jaxpr/convert_element_type | solution.py:115
  351.4 28.7 %dynamic_update_slice.41 = f32[2,512,12,64]{1,0,3,2:T(2,128)} dynamic-update-slice(f32[2,512,12,64]{1,0,3,2:T(2,128)} %get-tuple-element.759, f32[1,512,12,64]{1,0,3,2:T(1,128)S(1)} %copy.136, s32[]{:T(128)S(6)} %copy.153, s32[]{:T(128)} %constant.129.clone.1..sunk.1, s32[]{:T(128)} %constant.129.clone.1..sunk.1, s32[]{:T(128)} %constant.129.clone.1..sunk.1) | dynamic-update-slice | bytes 3145732 | tf_op jit(solution)/shard_map/while/body/eval_jaxpr/while/body/jit(dynamic_update_index_in_dim)/dynamic_update_slice | solution.py:136
  396.6 14.2 %bitcast_add_fusion.7 = f32[1024,12,64]{0,2,1:T(8,128)} fusion(f32[1024,12,64]{0,2,1:T(8,128)} %get-tuple-element.758, f32[12,512,1024]{2,1,0:T(8,128)} %fusion.141, f32[12,512]{1,0:T(8,128)S(1)} %dynamic-slice_bitcast_fusion.2, pred[512,1024]{1,0:T(8,128)(4,1)S(1)} %fusion.143, pred[]{:T(512)S(6)} %compare.3, ...), kind=kOutput, calls=%fused_computation.31.clone.1 | convolution fusion | flops 832045056 | bytes 32800772 | tf_op jit(solution)/shard_map/while/body/eval_jaxpr/while/body/eval_jaxpr/hqk,qhd->khd/dot_general | solution.py:127
  410.8 18.1 %multiply_reduce_fusion.9 = (f32[12,512]{1,0:T(8,128)S(1)}, f32[12,512,1024]{2,1,0:T(8,128)}) fusion(f32[12,512,1024]{2,1,0:T(8,128)} %fusion.141, f32[12,512]{1,0:T(8,128)S(1)} %dynamic-slice_bitcast_fusion.2, pred[512,1024]{1,0:T(8,128)(4,1)S(1)} %fusion.143, bf16[1024,12,64]{0,2,1:T(8,128)(2,1)} %get-tuple-element.784, ...), kind=kOutput, calls=%fused_computation.26.clone.1 | convolution fusion | flops 836757504 | bytes 53264388 | tf_op jit(solution)/shard_map/while/body/eval_jaxpr/while/body/eval_jaxpr/qhd,khd->hqk/dot_general | solution.py:111
  428.9 21.2 %multiply_convert_fusion.6 = bf16[12,512,1024]{2,1,0:T(8,128)(2,1)} fusion(f32[12,512,1024]{2,1,0:T(8,128)} %get-tuple-element.698, f32[12,512,1024]{2,1,0:T(8,128)} %fusion.141, f32[12,512]{1,0:T(8,128)S(1)} %get-tuple-element.699, f32[12,512]{1,0:T(8,128)S(1)} %dynamic-slice_bitcast_fusion.2, pred[512,1024]{1,0:T(8,128)(4,1)S(1)} %fusion.143), kind=kLoop, calls=%fused_computation.25.clone.1 | loop fusion | flops 37748736 | bytes 63488000 | tf_op jit(solution)/shard_map/while/body/eval_jaxpr/while/body/eval_jaxpr/convert_element_type | solution.py:115
  471.3 28.7 %dynamic_update_slice.41 = f32[2,512,12,64]{1,0,3,2:T(2,128)} dynamic-update-slice(f32[2,512,12,64]{1,0,3,2:T(2,128)} %get-tuple-element.759, f32[1,512,12,64]{1,0,3,2:T(1,128)S(1)} %copy.136, s32[]{:T(128)S(6)} %copy.153, s32[]{:T(128)} %constant.129.clone.1..sunk.1, s32[]{:T(128)} %constant.129.clone.1..sunk.1, s32[]{:T(128)} %constant.129.clone.1..sunk.1) | dynamic-update-slice | bytes 3145732 | tf_op jit(solution)/shard_map/while/body/eval_jaxpr/while/body/jit(dynamic_update_index_in_dim)/dynamic_update_slice | solution.py:136
  576.2 38.4 %psum.49 = f32[5]{0:T(128)} all-reduce(f32[5]{0:T(128)S(1)} %pad_maximum_fusion.7), channel_id=1, replica_groups=mesh['rep'=2,'shard'=16] {'rep','shard'}, use_global_device_ids=true, to_apply=%region_16.17 | all-reduce | flops 5 | bytes 40 | tf_op jit(solution)/shard_map/psum | solution.py:204
  616.2 51.8 %reduce-scatter.15.cloned.1.call-done = bf16[48,3072]{1,0:T(8,128)(2,1)} async-done(((bf16[768,3072]{1,0:T(8,128)(2,1)}), bf16[48,3072]{1,0:T(8,128)(2,1)}) %reduce-scatter.15.cloned.1.call-update) | async-done | bytes 294928 | tf_op jit(solution)/shard_map/reduce_scatter | solution.py:257
  667.9 78.5 %reduce-scatter.17.cloned.1.call-done = bf16[192,768]{1,0:T(8,128)(2,1)} async-done(((bf16[3072,768]{1,0:T(8,128)(2,1)}), bf16[192,768]{1,0:T(8,128)(2,1)}) %reduce-scatter.17.cloned.1.call-update) | async-done | bytes 294928 | tf_op jit(solution)/shard_map/reduce_scatter | solution.py:260
  755.5 47.6 %reduce-scatter.21.cloned.1.call-done = bf16[48,2]{1,0:T(8,128)(2,1)} async-done(((bf16[768,2]{1,0:T(8,128)(2,1)}), bf16[48,2]{1,0:T(8,128)(2,1)}) %reduce-scatter.21.cloned.1.call-update) | async-done | bytes 208
  803.9 55.5 %reduce-scatter.19.cloned.1.call-done = bf16[48,2]{1,0:T(8,128)(2,1)} async-done(((bf16[768,2]{1,0:T(8,128)(2,1)}), bf16[48,2]{1,0:T(8,128)(2,1)}) %reduce-scatter.19.cloned.1.call-update) | async-done | bytes 208
  866.2 31.3 %all-reduce.4.cloned.1.call-done = (bf16[48,2304]{1,0:T(8,128)(2,1)}, bf16[48,768]{1,0:T(8,128)(2,1)}, bf16[48,3072]{1,0:T(8,128)(2,1)}, bf16[192,768]{1,0:T(8,128)(2,1)}) async-done(((bf16[48,2304]{1,0:T(8,128)(2,1)}, bf16[48,768]{1,0:T(8,128)(2,1)}, bf16[48,3072]{1,0:T(8,128)(2,1)}, bf16[192,768]{1,0:T(8,128)(2,1)}), (bf16[48,2304]{1,0:T(8,128)(2,1)}, bf16[48,768]{1,0:T(8,128)(2,1)}, ...) | async-done | bytes 884752 | tf_op jit(solution)/shard_map/psum | solution.py:271
  (269 shorter events, 304.7 us)
Async XLA Ops:
  7.2 70.6 %all-gather.7.cloned.1.call-start = ((), (), s32[]{:S(2)}) async-start(), calls=%async_computation.6 | async-start | bytes 3760128 | tf_op jit(solution)/shard_map/all_gather | solution.py:162
  7.9 183.2 %all-gather.9.cloned.1.call-start = ((), (), s32[]{:S(2)}) async-start(), calls=%async_computation.7 | async-start | bytes 1253376 | tf_op jit(solution)/shard_map/all_gather | solution.py:163
  8.7 187.8 %all-gather.11.cloned.1.call-start = ((), (), s32[]{:S(2)}) async-start(), calls=%async_computation.8 | async-start | bytes 5013504 | tf_op jit(solution)/shard_map/all_gather | solution.py:164
  9.4 200.7 %all-gather.13.cloned.1.call-start = ((), (), s32[]{:S(2)}) async-start(), calls=%async_computation.9 | async-start | bytes 5013504 | tf_op jit(solution)/shard_map/all_gather | solution.py:165
  10.0 606.2 %reduce-scatter.13.cloned.1.call-start = ((), (), s32[]{:S(2)}) async-start(), calls=%async_computation.11 | async-start | bytes 1253376 | tf_op jit(solution)/shard_map/reduce_scatter | solution.py:254
  55.0 46.0 %copy-start.18 = (f32[1024,64]{0,1:T(8,128)}, f32[1024,64]{0,1:T(8,128)S(1)}, u32[]{:S(2)}) copy-start(f32[1024,64]{0,1:T(8,128)S(1)} %get-tuple-element.546) | copy-start | bytes 786436
  56.9 20.9 %copy-start.2 = (bf16[1024,768]{0,1:T(8,128)(2,1)}, bf16[1024,768]{0,1:T(8,128)(2,1)S(1)}, u32[]{:S(2)}) copy-start(bf16[1024,768]{0,1:T(8,128)(2,1)S(1)} %copy.80) | copy-start | bytes 4718596
  57.2 20.7 %copy-start.32 = (f32[1024]{0:T(1024)}, f32[1024]{0:T(1024)S(1)}, u32[]{:S(2)}) copy-start(f32[1024]{0:T(1024)S(1)} %broadcast_multiply_fusion.7) | copy-start | bytes 12292
  57.6 20.2 %copy-start.36 = (f32[1024]{0:T(1024)}, f32[1024]{0:T(1024)S(1)}, u32[]{:S(2)}) copy-start(f32[1024]{0:T(1024)S(1)} %add_rsqrt_fusion.1) | copy-start | bytes 12292
  91.2 9.5 %copy-start.5 = (f32[1024,768]{0,1:T(8,128)}, f32[1024,768]{0,1:T(8,128)S(1)}, u32[]{:S(2)}) copy-start(f32[1024,768]{0,1:T(8,128)S(1)} %copy.85) | copy-start | bytes 9437188
  194.5 43.9 %copy-start.38 = (f32[1024]{0:T(1024)}, f32[1024]{0:T(1024)S(1)}, u32[]{:S(2)}) copy-start(f32[1024]{0:T(1024)S(1)} %broadcast_multiply_fusion.6) | copy-start | bytes 12292
  196.5 41.9 %copy-start.42 = (f32[1024]{0:T(1024)}, f32[1024]{0:T(1024)S(1)}, u32[]{:S(2)}) copy-start(f32[1024]{0:T(1024)S(1)} %add_rsqrt_fusion) | copy-start | bytes 12292
  196.5 13.6 %copy-start.16 = (bf16[1024,768]{0,1:T(8,128)(2,1)S(1)}, bf16[1024,768]{0,1:T(8,128)(2,1)}, u32[]{:S(2)}) copy-start(bf16[1024,768]{0,1:T(8,128)(2,1)} %copy.90) | copy-start | bytes 4718596
  210.1 12.8 %copy-start.52 = (bf16[768,3072]{1,0:T(8,128)(2,1)S(1)}, bf16[768,3072]{1,0:T(8,128)(2,1)}, u32[]{:S(2)}) copy-start(bf16[768,3072]{1,0:T(8,128)(2,1)} %all-gather.11.cloned.1.call-done) | copy-start | bytes 14155780
  256.6 359.5 %reduce-scatter.11.cloned.1.call-start = ((), (), s32[]{:S(2)}) async-start(), calls=%async_computation.10 | async-start | bytes 3760128 | tf_op jit(solution)/shard_map/reduce_scatter | solution.py:251
  266.6 11.6 %copy-start.13 = (bf16[1024,12,64]{0,2,1:T(8,128)(2,1)S(1)}, bf16[1024,12,64]{0,2,1:T(8,128)(2,1)}, u32[]{:S(2)}) copy-start(bf16[1024,12,64]{0,2,1:T(8,128)(2,1)} %get-tuple-element.783) | copy-start | bytes 4718596 | tf_op jit(solution)/shard_map/while/body/eval_jaxpr/while
  385.1 11.5 %copy-start.13 = (bf16[1024,12,64]{0,2,1:T(8,128)(2,1)S(1)}, bf16[1024,12,64]{0,2,1:T(8,128)(2,1)}, u32[]{:S(2)}) copy-start(bf16[1024,12,64]{0,2,1:T(8,128)(2,1)} %get-tuple-element.783) | copy-start | bytes 4718596 | tf_op jit(solution)/shard_map/while/body/eval_jaxpr/while
  459.8 9.9 %copy-start.1 = (f32[1,512,12,64]{1,3,2,0:T(8,128)S(1)}, f32[1,512,12,64]{1,3,2,0:T(8,128)}, u32[]{:S(2)}) copy-start(f32[1,512,12,64]{1,3,2,0:T(8,128)} %multiply_bitcast_fusion.3) | copy-start | bytes 4718596 | tf_op jit(solution)/shard_map/while/body/eval_jaxpr/while
  522.8 145.1 %reduce-scatter.15.cloned.1.call-start = ((), (), s32[]{:S(2)}) async-start(), calls=%async_computation.12 | async-start | bytes 5013504 | tf_op jit(solution)/shard_map/reduce_scatter | solution.py:257
  533.3 213.2 %reduce-scatter.17.cloned.1.call-start = ((), (), s32[]{:S(2)}) async-start(), calls=%async_computation.13 | async-start | bytes 5013504 | tf_op jit(solution)/shard_map/reduce_scatter | solution.py:260
  545.7 257.4 %reduce-scatter.21.cloned.1.call-start = ((), (), s32[]{:S(2)}) async-start(), calls=%async_computation.15 | async-start | bytes 208896
  571.4 43.2 %copy-start.23 = (bf16[1024,768]{0,1:T(8,128)(2,1)S(1)}, bf16[1024,768]{0,1:T(8,128)(2,1)}, u32[]{:S(2)}) copy-start(bf16[1024,768]{0,1:T(8,128)(2,1)} %get-tuple-element.534) | copy-start | bytes 4718596
  574.5 284.9 %reduce-scatter.19.cloned.1.call-start = ((), (), s32[]{:S(2)}) async-start(), calls=%async_computation.14 | async-start | bytes 208896
  576.2 321.4 %all-reduce.4.cloned.1.call-start = ((), (), s32[]{:S(2)}) async-start(), calls=%async_computation.16 | async-start | bytes 1769472 | tf_op jit(solution)/shard_map/psum | solution.py:271
  (45 other events, 155.1 us)
Sparse Core Ops, SparseCore 0:
  10.3 49.9 all-gather.6
  62.5 36.9 all-gather.8
  101.7 51.9 all-gather.10
  155.9 51.6 all-gather.12
  256.8 56.7 reduce-scatter.12
  522.9 66.7 reduce-scatter.10
  593.5 74.3 reduce-scatter.14
  671.8 74.6 reduce-scatter.16
  750.6 52.4 reduce-scatter.20
  807.0 52.3 reduce-scatter.18
  861.9 35.5 all-reduce.3
where the time goes:
time: 926 us; the launch traced here: 911 us
  matrix products  279 us (30%)
  waiting for transfers between devices  267 us (29%)
  local copies, waits for them, and re-layouts  133 us (14%)
  other arithmetic  125 us (13%)
  blocking collectives  84.4 us (9%)
  between operations  15.7 us (2%)
    unnamed x13, waiting for transfers between devices  106 us
    reduce_scatter x1, waiting for transfers between devices, local(): lax.psum_scatter(local_grads[3].astype(jnp.bfloat16), 'shard', scatter_di...  78.5 us
    dynamic_update_slice x4, local copies, waits for them, and re-layouts, attend_backward(): lax.scan(one_block, (zero_rows, zero_rows), jnp.arange(block_count, dtype...  60.6 us
    reduce_scatter x1, waiting for transfers between devices, local(): lax.psum_scatter(local_grads[2].astype(jnp.bfloat16), 'shard', scatter_di...  51.8 us
    dot_general x4, matrix products, block_scores(): jnp.einsum('qhd,khd->hqk', query_block, key_rows, preferred_element_type=...  47.1 us
    convert_element_type x2, other arithmetic, one_block(): grad_scores = (attn_probs * (grad_probs - delta_sum)).astype(jnp.bfloat16)  42.5 us
    psum x1, blocking collectives, local(): grad_mix = lax.psum(partial_mix, ('rep', 'shard'))  38.4 us
    dot_general x2, matrix products, one_block(): jnp.einsum('qhd,khd->hqk', grad_block, value_rows, preferred_element_type...  36.3 us
  transfers between devices with their start and end apart: 11, of which 5 were waited for; matrix products, arithmetic and copies ran while one was open for 52% of the time, Pallas kernels for 0%

commit v1 on v0

--- a/solution.py
+++ b/solution.py
@@ -268,7 +268,9 @@
         ).astype(jnp.float32),
     )
     owned = (
-        lax.psum(owned[0].astype(jnp.bfloat16), "rep").astype(jnp.float32),
+        jnp.sum(lax.all_gather(owned[0].astype(jnp.bfloat16), axis_name="rep"), 0).astype(
+            jnp.float32
+        ),
         lax.psum(owned[1].astype(jnp.bfloat16), "rep").astype(jnp.float32),
         lax.psum(owned[2].astype(jnp.bfloat16), "rep").astype(jnp.float32),
         lax.psum(owned[3].astype(jnp.bfloat16), "rep").astype(jnp.float32),

time: 926 us -> 795 us (0.86)
  waiting for transfers between devices: 267 us -> 128 us
    reduce_scatter x1, waiting for transfers between devices: 78.5 us -> 0.02 us  [local(): lax.psum_scatter(local_grads[3].astype(jnp.bfloat16), 'shard', scatter_di...]
    unnamed x13, waiting for transfers between devices: 106 us -> 37.9 us
    reduce_scatter x1, waiting for transfers between devices: 0.01 us -> 64.1 us  [local(): lax.psum_scatter(local_grads[0].astype(jnp.bfloat16), 'shard', scatter_di...]
    reduce_scatter x1, waiting for transfers between devices: 51.8 us -> 0.01 us  [local(): lax.psum_scatter(local_grads[2].astype(jnp.bfloat16), 'shard', scatter_di...]
    unnamed x118 -> x98, local copies, waits for them, and re-layouts: 27.2 us -> 26.6 us
  transfers between devices with their start and end apart: 11 -> 11, of which waited for: 5 -> 3; matrix products, arithmetic and copies ran while one was open for 52% -> 61% of each run, Pallas kernels for 0% -> 0%
where the time goes in v1:
time: 795 us; the launch traced here: 781 us
  matrix products  281 us (35%)
  local copies, waits for them, and re-layouts  132 us (17%)
  waiting for transfers between devices  128 us (16%)
  other arithmetic  124 us (16%)
  blocking collectives  91.6 us (12%)
  between operations  15.3 us (2%)
    reduce_scatter x1, waiting for transfers between devices, local(): lax.psum_scatter(local_grads[0].astype(jnp.bfloat16), 'shard', scatter_di...  64.1 us
    dynamic_update_slice x4, local copies, waits for them, and re-layouts, attend_backward(): lax.scan(one_block, (zero_rows, zero_rows), jnp.arange(block_count, dtype...  60.9 us
    dot_general x4, matrix products, block_scores(): jnp.einsum('qhd,khd->hqk', query_block, key_rows, preferred_element_type=...  46.9 us
    convert_element_type x2, other arithmetic, one_block(): grad_scores = (attn_probs * (grad_probs - delta_sum)).astype(jnp.bfloat16)  44.5 us
    psum x1, blocking collectives, local(): grad_mix = lax.psum(partial_mix, ('rep', 'shard'))  38.7 us
    unnamed x13, waiting for transfers between devices  37.9 us
    dot_general x2, matrix products, one_block(): jnp.einsum('qhd,khd->hqk', grad_block, value_rows, preferred_element_type...  37 us
    dot_general x2, matrix products, one_block(): jnp.einsum('hqk,qhd->khd', attn_probs.astype(jnp.bfloat16), grad_block, p...  28.3 us
  transfers between devices with their start and end apart: 11, of which 3 were waited for; matrix products, arithmetic and copies ran while one was open for 61% of the time, Pallas kernels for 0%

profile of v1, /device:TPU:0, one launch (start us, length us, event | category | flops | bytes accessed | tf_op | source)
XLA Modules:
  0.0 780.6 jit_solution(17351879389953660098)
XLA Ops:
  11.9 23.4 %all-gather.1 = bf16[16,48,2]{1,2,0:T(2,128)(2,1)S(1)} all-gather(bf16[1,48,2]{1,2,0:T(2,128)(2,1)} %bitcast.172), channel_id=1, replica_groups=mesh['rep'=2,'shard'=16] {'shard'}, dimensions={0}, use_global_device_ids=true | all-gather | bytes 3264 | tf_op jit(solution)/shard_map/all_gather | solution.py:166
  35.5 17.7 %all-gather.2 = bf16[16,48,2]{1,2,0:T(2,128)(2,1)S(1)} all-gather(bf16[1,48,2]{1,2,0:T(2,128)(2,1)} %bitcast.173), channel_id=1, replica_groups=mesh['rep'=2,'shard'=16] {'shard'}, dimensions={0}, use_global_device_ids=true | all-gather | bytes 3264 | tf_op jit(solution)/shard_map/all_gather | solution.py:167
  106.8 77.9 %while.52 = (s32[]{:T(128)}, bf16[2,512,12,64]{1,3,2,0:T(8,128)(2,1)S(1)}, f32[2,12,512]{2,1,0:T(8,128)S(1)}, s32[2]{0:T(128)S(1)}, s32[]{:T(128)}, /*index=5*/s...) while((s32[]{:T(128)}, ...), condition=%wide.region_5.6_spmd.clone.clone, body=%wide.region_2.5_spmd.clone.clone.sunk | while | flops 1681784320 | bytes 82558176 | solution.py:92
  109.9 12.0 %fusion.130 = (f32[12,512]{1,0:T(8,128)S(1)}, f32[12,512,1024]{2,1,0:T(8,128)}) fusion(pred[512,1024]{1,0:T(8,128)(4,1)S(1)} %fusion.129, bf16[1024,12,64]{0,2,1:T(8,128)(2,1)S(1)} %get-tuple-element.732, bf16[1024,12,64]{0,2,1:T(8,128)(2,1)} %get-tuple-element.731, s32[]{:T(128)S(6)} %select_n.68), kind=kOutput, calls=%fused_computation.5.clone.1 | convolution fusion | flops 824174592 | bytes 28073988 | tf_op jit(solution)/shard_map/while/body/eval_jaxpr/while/body/eval_jaxpr/qhd,khd->hqk/dot_general | solution.py:67
  121.9 12.1 %exponential_reduce_fusion.2 = f32[12,512]{1,0:T(8,128)S(1)} fusion(f32[12,512,1024]{2,1,0:T(8,128)} %get-tuple-element.681, f32[12,512]{1,0:T(8,128)S(1)} %get-tuple-element.682, pred[512,1024]{1,0:T(8,128)(4,1)S(1)} %fusion.129), kind=kLoop, calls=%fused_computation.3.clone.1 | loop fusion | flops 25159680 | bytes 25739264 | tf_op jit(solution)/shard_map/while/body/eval_jaxpr/while/body/eval_jaxpr/reduce_sum | solution.py:85
  134.0 11.8 %fusion.131 = bf16[2,512,12,64]{1,3,2,0:T(8,128)(2,1)S(1)} fusion(bf16[2,512,12,64]{1,3,2,0:T(8,128)(2,1)S(1)} %get-tuple-element.713, s32[]{:T(128)S(6)} %copy.143, bf16[1024,12,64]{0,2,1:T(8,128)(2,1)} %get-tuple-element.733, f32[12,512,1024]{2,1,0:T(8,128)} %get-tuple-element.681, f32[12,512]{1,0:T(8,128)S(1)} %get-tuple-element.683, ...), kind=kOutput, calls=%fused_computation.12.clone.1 | convolution fusion | flops 830865408 | bytes 28082180 | tf_op jit(solution)/shard_map/while/body/eval_jaxpr/while/body/eval_jaxpr/hqk,khd->qhd/dot_general | solution.py:87
  148.9 11.9 %fusion.130 = (f32[12,512]{1,0:T(8,128)S(1)}, f32[12,512,1024]{2,1,0:T(8,128)}) fusion(pred[512,1024]{1,0:T(8,128)(4,1)S(1)} %fusion.129, bf16[1024,12,64]{0,2,1:T(8,128)(2,1)S(1)} %get-tuple-element.732, bf16[1024,12,64]{0,2,1:T(8,128)(2,1)} %get-tuple-element.731, s32[]{:T(128)S(6)} %select_n.68), kind=kOutput, calls=%fused_computation.5.clone.1 | convolution fusion | flops 824174592 | bytes 28073988 | tf_op jit(solution)/shard_map/while/body/eval_jaxpr/while/body/eval_jaxpr/qhd,khd->hqk/dot_general | solution.py:67
  160.8 12.0 %exponential_reduce_fusion.2 = f32[12,512]{1,0:T(8,128)S(1)} fusion(f32[12,512,1024]{2,1,0:T(8,128)} %get-tuple-element.681, f32[12,512]{1,0:T(8,128)S(1)} %get-tuple-element.682, pred[512,1024]{1,0:T(8,128)(4,1)S(1)} %fusion.129), kind=kLoop, calls=%fused_computation.3.clone.1 | loop fusion | flops 25159680 | bytes 25739264 | tf_op jit(solution)/shard_map/while/body/eval_jaxpr/while/body/eval_jaxpr/reduce_sum | solution.py:85
  196.0 13.5 %multiply_convert_fusion.1 = (bf16[1024,3072]{1,0:T(8,128)(2,1)}, f32[1024,3072]{1,0:T(8,128)}) fusion(bf16[768,3072]{1,0:T(8,128)(2,1)} %all-gather.12.cloned.1.call-done, f32[1024,768]{0,1:T(8,128)} %copy-done.7, f32[768]{0:T(1024)S(1)} %copy-done.38, f32[768]{0:T(1024)S(1)} %copy-done.34, f32[1024]{0:T(1024)S(1)} %add_rsqrt_fusion, ...), kind=kOutput, calls=%fused_computation.62 | convolution fusion | flops 4851499008 | bytes 26753024 | tf_op jit(solution)/shard_map/dot_general | solution.py:194
  209.5 13.1 %fusion.42 = bf16[1024,3072]{1,0:T(8,128)(2,1)S(1)} fusion(f32[1024,3072]{1,0:T(8,128)} %get-tuple-element.552, bf16[3072,768]{1,0:T(8,128)(2,1)} %all-gather.14.cloned.1.call-done, bf16[1024,768]{0,1:T(8,128)(2,1)S(1)} %copy-done.16, f32[]{:T(128)} %bitcast.4), kind=kOutput, calls=%fused_computation.60 | convolution fusion | flops 4865654784 | bytes 25165828 | tf_op jit(solution)/shard_map/td,fd->tf/dot_general | solution.py:214
  238.2 12.5 %multiply_reduce_fusion.3 = (f32[]{:T(128)}, bf16[1024,768]{0,1:T(8,128)(2,1)}, f32[1024,768]{0,1:T(8,128)S(1)}) fusion(bf16[1024,768]{0,1:T(8,128)(2,1)S(1)} %copy-done.16, f32[]{:T(128)} %bitcast.4, f32[1,1024,768]{1,2,0:T(8,128)} %copy.101, f32[1024]{0:T(1024)S(1)} %broadcast_multiply_fusion.4, f32[1024,768]{0,1:T(8,128)S(1)} %copy-done.8, ...), kind=kOutput, calls=%fused_computation.104 | convolution fusion | flops 4844421120 | bytes 26758152 | tf_op jit(solution)/shard_map/dot_general | solution.py:197
  282.7 242.5 %while.53 = (s32[]{:T(128)}, f32[1024,12,64]{0,2,1:T(8,128)}, f32[1024,12,64]{0,2,1:T(8,128)}, f32[2,512,12,64]{1,0,3,2:T(2,128)}, s32[2]{0:T(128)S(1)}, /*index...) while((s32[]{:T(128)}, f32[1024,12,64]{0,2,1:T(8,128)}, ...), condition=%wide.region_12.13_spmd.clone.clone, body=%wide.region_10.12_spmd.clone.clone.sunk | while | flops 4126801408 | bytes 231923056 | solution.py:136
  299.3 13.5 %bitcast_add_fusion.7 = f32[1024,12,64]{0,2,1:T(8,128)} fusion(f32[1024,12,64]{0,2,1:T(8,128)} %get-tuple-element.757, f32[12,512,1024]{2,1,0:T(8,128)} %fusion.141, f32[12,512]{1,0:T(8,128)S(1)} %dynamic-slice_bitcast_fusion.2, pred[512,1024]{1,0:T(8,128)(4,1)S(1)} %fusion.143, pred[]{:T(512)S(6)} %compare.3, ...), kind=kOutput, calls=%fused_computation.31.clone.1 | convolution fusion | flops 832045056 | bytes 32800772 | tf_op jit(solution)/shard_map/while/body/eval_jaxpr/while/body/eval_jaxpr/hqk,qhd->khd/dot_general | solution.py:127
  312.7 18.9 %multiply_reduce_fusion.9 = (f32[12,512]{1,0:T(8,128)S(1)}, f32[12,512,1024]{2,1,0:T(8,128)}) fusion(f32[12,512,1024]{2,1,0:T(8,128)} %fusion.141, f32[12,512]{1,0:T(8,128)S(1)} %dynamic-slice_bitcast_fusion.2, pred[512,1024]{1,0:T(8,128)(4,1)S(1)} %fusion.143, bf16[1024,12,64]{0,2,1:T(8,128)(2,1)} %get-tuple-element.783, ...), kind=kOutput, calls=%fused_computation.26.clone.1 | convolution fusion | flops 836757504 | bytes 53264388 | tf_op jit(solution)/shard_map/while/body/eval_jaxpr/while/body/eval_jaxpr/qhd,khd->hqk/dot_general | solution.py:111
  331.6 22.8 %multiply_convert_fusion.6 = bf16[12,512,1024]{2,1,0:T(8,128)(2,1)} fusion(f32[12,512,1024]{2,1,0:T(8,128)} %get-tuple-element.697, f32[12,512,1024]{2,1,0:T(8,128)} %fusion.141, f32[12,512]{1,0:T(8,128)S(1)} %get-tuple-element.698, f32[12,512]{1,0:T(8,128)S(1)} %dynamic-slice_bitcast_fusion.2, pred[512,1024]{1,0:T(8,128)(4,1)S(1)} %fusion.143), kind=kLoop, calls=%fused_computation.25.clone.1 | loop fusion | flops 37748736 | bytes 63488000 | tf_op jit(solution)/shard_map/while/body/eval_jaxpr/while/body/eval_jaxpr/convert_element_type | solution.py:115
  374.7 28.8 %dynamic_update_slice.41 = f32[2,512,12,64]{1,0,3,2:T(2,128)} dynamic-update-slice(f32[2,512,12,64]{1,0,3,2:T(2,128)} %get-tuple-element.758, f32[1,512,12,64]{1,0,3,2:T(1,128)S(1)} %copy.136, s32[]{:T(128)S(6)} %copy.153, s32[]{:T(128)} %constant.130.clone.1..sunk.1, s32[]{:T(128)} %constant.130.clone.1..sunk.1, s32[]{:T(128)} %constant.130.clone.1..sunk.1) | dynamic-update-slice | bytes 3145732 | tf_op jit(solution)/shard_map/while/body/eval_jaxpr/while/body/jit(dynamic_update_index_in_dim)/dynamic_update_slice | solution.py:136
  420.1 14.9 %bitcast_add_fusion.7 = f32[1024,12,64]{0,2,1:T(8,128)} fusion(f32[1024,12,64]{0,2,1:T(8,128)} %get-tuple-element.757, f32[12,512,1024]{2,1,0:T(8,128)} %fusion.141, f32[12,512]{1,0:T(8,128)S(1)} %dynamic-slice_bitcast_fusion.2, pred[512,1024]{1,0:T(8,128)(4,1)S(1)} %fusion.143, pred[]{:T(512)S(6)} %compare.3, ...), kind=kOutput, calls=%fused_computation.31.clone.1 | convolution fusion | flops 832045056 | bytes 32800772 | tf_op jit(solution)/shard_map/while/body/eval_jaxpr/while/body/eval_jaxpr/hqk,qhd->khd/dot_general | solution.py:127
  435.0 18.1 %multiply_reduce_fusion.9 = (f32[12,512]{1,0:T(8,128)S(1)}, f32[12,512,1024]{2,1,0:T(8,128)}) fusion(f32[12,512,1024]{2,1,0:T(8,128)} %fusion.141, f32[12,512]{1,0:T(8,128)S(1)} %dynamic-slice_bitcast_fusion.2, pred[512,1024]{1,0:T(8,128)(4,1)S(1)} %fusion.143, bf16[1024,12,64]{0,2,1:T(8,128)(2,1)} %get-tuple-element.783, ...), kind=kOutput, calls=%fused_computation.26.clone.1 | convolution fusion | flops 836757504 | bytes 53264388 | tf_op jit(solution)/shard_map/while/body/eval_jaxpr/while/body/eval_jaxpr/qhd,khd->hqk/dot_general | solution.py:111
  453.1 21.8 %multiply_convert_fusion.6 = bf16[12,512,1024]{2,1,0:T(8,128)(2,1)} fusion(f32[12,512,1024]{2,1,0:T(8,128)} %get-tuple-element.697, f32[12,512,1024]{2,1,0:T(8,128)} %fusion.141, f32[12,512]{1,0:T(8,128)S(1)} %get-tuple-element.698, f32[12,512]{1,0:T(8,128)S(1)} %dynamic-slice_bitcast_fusion.2, pred[512,1024]{1,0:T(8,128)(4,1)S(1)} %fusion.143), kind=kLoop, calls=%fused_computation.25.clone.1 | loop fusion | flops 37748736 | bytes 63488000 | tf_op jit(solution)/shard_map/while/body/eval_jaxpr/while/body/eval_jaxpr/convert_element_type | solution.py:115
  496.0 28.8 %dynamic_update_slice.41 = f32[2,512,12,64]{1,0,3,2:T(2,128)} dynamic-update-slice(f32[2,512,12,64]{1,0,3,2:T(2,128)} %get-tuple-element.758, f32[1,512,12,64]{1,0,3,2:T(1,128)S(1)} %copy.136, s32[]{:T(128)S(6)} %copy.153, s32[]{:T(128)} %constant.130.clone.1..sunk.1, s32[]{:T(128)} %constant.130.clone.1..sunk.1, s32[]{:T(128)} %constant.130.clone.1..sunk.1) | dynamic-update-slice | bytes 3145732 | tf_op jit(solution)/shard_map/while/body/eval_jaxpr/while/body/jit(dynamic_update_index_in_dim)/dynamic_update_slice | solution.py:136
  579.2 38.7 %psum.42 = f32[5]{0:T(128)} all-reduce(f32[5]{0:T(128)S(1)} %pad_maximum_fusion.7), channel_id=1, replica_groups=mesh['rep'=2,'shard'=16] {'rep','shard'}, use_global_device_ids=true, to_apply=%region_16.17 | all-reduce | flops 5 | bytes 40 | tf_op jit(solution)/shard_map/psum | solution.py:204
  629.4 35.2 %reduce-scatter.19.cloned.1.call-done = bf16[48,2]{1,0:T(8,128)(2,1)} async-done(((bf16[768,2]{1,0:T(8,128)(2,1)}), bf16[48,2]{1,0:T(8,128)(2,1)}) %reduce-scatter.19.cloned.1.call-update) | async-done | bytes 208
  671.4 64.1 %reduce-scatter.11.cloned.1.call-done = bf16[48,2304]{1,0:T(8,128)(2,1)} async-done(((bf16[768,2304]{1,0:T(8,128)(2,1)}), bf16[48,2304]{1,0:T(8,128)(2,1)}) %reduce-scatter.11.cloned.1.call-update) | async-done | bytes 221200 | tf_op jit(solution)/shard_map/reduce_scatter | solution.py:251
  743.2 25.5 %all-reduce.4.cloned.1.call-done = (bf16[48,768]{1,0:T(8,128)(2,1)}, bf16[48,3072]{1,0:T(8,128)(2,1)}, bf16[192,768]{1,0:T(8,128)(2,1)}) async-done(((bf16[48,768]{1,0:T(8,128)(2,1)}, bf16[48,3072]{1,0:T(8,128)(2,1)}, bf16[192,768]{1,0:T(8,128)(2,1)}), (bf16[48,768]{1,0:T(8,128)(2,1)}, bf16[48,3072]{1,0:T(8,128)(2,1)}, bf16[192,768]{1,0:T(8,128)(2,1)})) %all-reduce.4.cloned.1.call-update) | async-done | bytes 663568 | tf_op jit(solution)/shard_map/psum | solution.py:274
  (251 shorter events, 286.7 us)
Async XLA Ops:
  7.2 70.6 %all-gather.8.cloned.1.call-start = ((), (), s32[]{:S(2)}) async-start(), calls=%async_computation.6 | async-start | bytes 3760128 | tf_op jit(solution)/shard_map/all_gather | solution.py:162
  7.9 182.7 %all-gather.10.cloned.1.call-start = ((), (), s32[]{:S(2)}) async-start(), calls=%async_computation.7 | async-start | bytes 1253376 | tf_op jit(solution)/shard_map/all_gather | solution.py:163
  8.7 187.3 %all-gather.12.cloned.1.call-start = ((), (), s32[]{:S(2)}) async-start(), calls=%async_computation.8 | async-start | bytes 5013504 | tf_op jit(solution)/shard_map/all_gather | solution.py:164
  9.4 200.1 %all-gather.14.cloned.1.call-start = ((), (), s32[]{:S(2)}) async-start(), calls=%async_computation.9 | async-start | bytes 5013504 | tf_op jit(solution)/shard_map/all_gather | solution.py:165
  10.0 609.5 %reduce-scatter.13.cloned.1.call-start = ((), (), s32[]{:S(2)}) async-start(), calls=%async_computation.11 | async-start | bytes 1253376 | tf_op jit(solution)/shard_map/reduce_scatter | solution.py:254
  55.0 45.9 %copy-start.17 = (f32[1024,64]{0,1:T(8,128)}, f32[1024,64]{0,1:T(8,128)S(1)}, u32[]{:S(2)}) copy-start(f32[1024,64]{0,1:T(8,128)S(1)} %get-tuple-element.545) | copy-start | bytes 786436
  56.9 20.9 %copy-start.2 = (bf16[1024,768]{0,1:T(8,128)(2,1)}, bf16[1024,768]{0,1:T(8,128)(2,1)S(1)}, u32[]{:S(2)}) copy-start(bf16[1024,768]{0,1:T(8,128)(2,1)S(1)} %copy.80) | copy-start | bytes 4718596
  57.2 20.6 %copy-start.28 = (f32[1024]{0:T(1024)}, f32[1024]{0:T(1024)S(1)}, u32[]{:S(2)}) copy-start(f32[1024]{0:T(1024)S(1)} %broadcast_multiply_fusion.7) | copy-start | bytes 12292
  57.6 20.2 %copy-start.32 = (f32[1024]{0:T(1024)}, f32[1024]{0:T(1024)S(1)}, u32[]{:S(2)}) copy-start(f32[1024]{0:T(1024)S(1)} %add_rsqrt_fusion.1) | copy-start | bytes 12292
  91.1 9.5 %copy-start.5 = (f32[1024,768]{0,1:T(8,128)}, f32[1024,768]{0,1:T(8,128)S(1)}, u32[]{:S(2)}) copy-start(f32[1024,768]{0,1:T(8,128)S(1)} %copy.85) | copy-start | bytes 9437188
  196.0 13.5 %copy-start.16 = (bf16[1024,768]{0,1:T(8,128)(2,1)S(1)}, bf16[1024,768]{0,1:T(8,128)(2,1)}, u32[]{:S(2)}) copy-start(bf16[1024,768]{0,1:T(8,128)(2,1)} %copy.90) | copy-start | bytes 4718596
  209.5 13.1 %copy-start.42 = (bf16[768,3072]{1,0:T(8,128)(2,1)S(1)}, bf16[768,3072]{1,0:T(8,128)(2,1)}, u32[]{:S(2)}) copy-start(bf16[768,3072]{1,0:T(8,128)(2,1)} %all-gather.12.cloned.1.call-done) | copy-start | bytes 14155780
  256.3 363.2 %reduce-scatter.15.cloned.1.call-start = ((), (), s32[]{:S(2)}) async-start(), calls=%async_computation.12 | async-start | bytes 5013504 | tf_op jit(solution)/shard_map/reduce_scatter | solution.py:257
  266.2 353.3 %reduce-scatter.17.cloned.1.call-start = ((), (), s32[]{:S(2)}) async-start(), calls=%async_computation.13 | async-start | bytes 5013504 | tf_op jit(solution)/shard_map/reduce_scatter | solution.py:260
  276.8 351.7 %reduce-scatter.21.cloned.1.call-start = ((), (), s32[]{:S(2)}) async-start(), calls=%async_computation.15 | async-start | bytes 208896
  282.7 242.5 %copy-start.39 = (bf16[768]{0:T(1024)(128)(2,1)S(1)}, bf16[768]{0:T(1024)(128)(2,1)}, u32[]{:S(2)}) copy-start(bf16[768]{0:T(1024)(128)(2,1)} %get-tuple-element.553) | copy-start | bytes 4612
  282.7 242.6 %copy-start.35 = (bf16[768]{0:T(1024)(128)(2,1)S(1)}, bf16[768]{0:T(1024)(128)(2,1)}, u32[]{:S(2)}) copy-start(bf16[768]{0:T(1024)(128)(2,1)} %get-tuple-element.467) | copy-start | bytes 4612
  287.9 11.4 %copy-start.13 = (bf16[1024,12,64]{0,2,1:T(8,128)(2,1)S(1)}, bf16[1024,12,64]{0,2,1:T(8,128)(2,1)}, u32[]{:S(2)}) copy-start(bf16[1024,12,64]{0,2,1:T(8,128)(2,1)} %get-tuple-element.782) | copy-start | bytes 4718596 | tf_op jit(solution)/shard_map/while/body/eval_jaxpr/while
  408.5 11.6 %copy-start.13 = (bf16[1024,12,64]{0,2,1:T(8,128)(2,1)S(1)}, bf16[1024,12,64]{0,2,1:T(8,128)(2,1)}, u32[]{:S(2)}) copy-start(bf16[1024,12,64]{0,2,1:T(8,128)(2,1)} %get-tuple-element.782) | copy-start | bytes 4718596 | tf_op jit(solution)/shard_map/while/body/eval_jaxpr/while
  484.6 9.8 %copy-start.1 = (f32[1,512,12,64]{1,3,2,0:T(8,128)S(1)}, f32[1,512,12,64]{1,3,2,0:T(8,128)}, u32[]{:S(2)}) copy-start(f32[1,512,12,64]{1,3,2,0:T(8,128)} %multiply_bitcast_fusion.3) | copy-start | bytes 4718596 | tf_op jit(solution)/shard_map/while/body/eval_jaxpr/while
  555.1 109.5 %reduce-scatter.19.cloned.1.call-start = ((), (), s32[]{:S(2)}) async-start(), calls=%async_computation.14 | async-start | bytes 208896
  556.0 179.5 %reduce-scatter.11.cloned.1.call-start = ((), (), s32[]{:S(2)}) async-start(), calls=%async_computation.10 | async-start | bytes 3760128 | tf_op jit(solution)/shard_map/reduce_scatter | solution.py:251
  564.0 204.7 %all-reduce.4.cloned.1.call-start = ((), (), s32[]{:S(2)}) async-start(), calls=%async_computation.16 | async-start | bytes 1327104 | tf_op jit(solution)/shard_map/psum | solution.py:274
  573.3 44.6 %copy-start.22 = (bf16[1024,768]{0,1:T(8,128)(2,1)S(1)}, bf16[1024,768]{0,1:T(8,128)(2,1)}, u32[]{:S(2)}) copy-start(bf16[1024,768]{0,1:T(8,128)(2,1)} %get-tuple-element.533) | copy-start | bytes 4718596
  (35 other events, 124.9 us)
Sparse Core Ops, SparseCore 0:
  10.3 49.9 all-gather.7
  62.5 36.9 all-gather.9
  101.7 52.0 all-gather.11
  155.9 51.7 all-gather.13
  256.4 56.6 reduce-scatter.12
  316.7 74.6 reduce-scatter.14
  395.2 74.7 reduce-scatter.16
  555.2 52.9 reduce-scatter.20
  612.2 52.3 reduce-scatter.18
  668.3 67.1 reduce-scatter.10
  737.9 30.6 all-reduce.3
